TPU v7x, 32 devices: a whole 2x2x4 slice. The times are simulated.
32 devices in a mesh: parts: 2 (over x), ctx: 4 (over z), branch: 4 (over y, core).
Axes of the slice: x: 2, y: 2, z: 4, core: 2. Of those that a mesh axis runs over, the one named last changes fastest.
Arguments:
- prefix_kv: bfloat16 [2, 8192, 1024], P(None, ('parts', 'ctx')), parts along dimension 1
- queries: bfloat16 [512, 8192], P(('parts', 'ctx', 'branch')), parts along dimension 0
- new_kv: bfloat16 [2, 512, 1024], P(None, ('parts', 'ctx', 'branch')), parts along dimension 1, may hold values from -6 to 6
- suffix_kv: bfloat16 [2, 512, 64, 1024], P(None, ('parts', 'ctx', 'branch')), parts along dimension 1, may hold values from -6 to 6
- suffix_len: int32 [512], P(('parts', 'ctx', 'branch')), parts along dimension 0, may hold values from 1 to 64, as said below
- node_kv: bfloat16 [2, 8, 128, 1024], P(None, ('parts', 'branch')), parts along dimension 1, may hold values from -6 to 6
- node_len: int32 [8], P('parts'), parts along dimension 0, may hold values from 1 to 128, as said below
- parent: int32 [8], P('parts'), parts along dimension 0, may hold values from -1 to 2, as said below
- leaf: int32 [512], P(('parts', 'ctx', 'branch')), parts along dimension 0, may hold values from 0 to 3
Outputs:
- context: bfloat16 [512, 8192], P(('parts', 'ctx', 'branch')), parts along dimension 0
There are 2 independent parts, one for each index of `parts`. A program takes and returns all parts, laid end to end along the dimension named above; each array names one. Nothing has to cross between parts.
Inputs may be any that keep to these rules, and one draw needn't show every extreme that they name: `suffix_len`: live tokens stand first in a rollout's suffix; some rollout has all 64. `node_len`: live tokens stand first in a node; some node has all 128. parent[n] is -1 or a node below n; parent[0] is -1.
All inputs are finite; a program needn't handle non-finite values.
Results may differ from a plain program's by a relative error of at most 0.0055.
Values may be sent and summed in bfloat16 or wider, within the bound.
A program may use at most 128 MiB of HBM per device.

v0:
```python
import math
import jax
import jax.numpy as jnp
from jax import lax
from jax.sharding import PartitionSpec as P

HEADS = 64
KV_HEADS = 8
HEAD_DIM = 128
NODE_LEN = 128


def attend(query_block, key_rows, value_rows, live_mask):
    scores = jnp.einsum("bhgd,thd->bhgt", query_block, key_rows, preferred_element_type=jnp.float32)
    scores = scores * query_block.shape[-1] ** (-0.5)
    if live_mask is not None:
        scores = jnp.where(live_mask[:, None, None, :], scores, -jnp.inf)
    maxima = jnp.max(scores, axis=-1)
    anchor = jnp.where(jnp.isfinite(maxima), maxima, 0.0)
    weights = jnp.exp(scores - anchor[..., None])
    totals = jnp.sum(weights, axis=-1)
    mixed = jnp.einsum(
        "bhgt,thd->bhgd",
        weights.astype(jnp.bfloat16),
        value_rows,
        preferred_element_type=jnp.float32,
    )
    return (mixed, maxima, totals)


def combine(first, second):
    mixed_a, maxima_a, totals_a = first
    mixed_b, maxima_b, totals_b = second
    maxima = jnp.maximum(maxima_a, maxima_b)
    anchor = jnp.where(jnp.isfinite(maxima), maxima, 0.0)
    scale_a = jnp.exp(maxima_a - anchor)
    scale_b = jnp.exp(maxima_b - anchor)
    mixed = mixed_a * scale_a[..., None] + mixed_b * scale_b[..., None]
    return (mixed, maxima, totals_a * scale_a + totals_b * scale_b)


def merge_parts(back_mixed, back_maxima, back_totals, ctx_size, rollouts, group):
    back_mixed = back_mixed.reshape(ctx_size, rollouts, KV_HEADS, group, HEAD_DIM)
    back_maxima = back_maxima.reshape(ctx_size, rollouts, KV_HEADS, group)
    back_totals = back_totals.reshape(ctx_size, rollouts, KV_HEADS, group)
    peak = jnp.max(back_maxima, axis=0)
    factors = jnp.exp(back_maxima - peak[None])
    return (
        jnp.sum(back_mixed * factors[..., None], axis=0),
        peak,
        jnp.sum(back_totals * factors, axis=0),
    )


def on_device(prefix_kv, queries, new_kv, suffix_kv, suffix_len, node_kv, node_len, parent, leaf):
    rollouts = queries.shape[0]
    group = HEADS // KV_HEADS
    inverse_root = HEAD_DIM ** (-0.5)
    query_heads = queries.reshape(rollouts, KV_HEADS, group, HEAD_DIM)
    prefix_keys = prefix_kv[0].reshape(-1, KV_HEADS, HEAD_DIM)
    prefix_values = prefix_kv[1].reshape(-1, KV_HEADS, HEAD_DIM)
    node_count = node_len.shape[0]
    node_ids = jnp.arange(node_count, dtype=jnp.int32)
    token_ids = jnp.arange(NODE_LEN, dtype=jnp.int32)
    ctx_size = lax.axis_size("ctx")
    query_rows = lax.all_gather(queries, "ctx", axis=0, tiled=True)
    count = query_rows.shape[0]
    width = math.gcd(count, 16)
    blocks = query_rows.reshape(count // width, width, KV_HEADS, group, HEAD_DIM)

    def one_block(block_rows):
        return attend(block_rows, prefix_keys, prefix_values, None)

    mixed, maxima, totals = lax.map(one_block, blocks)
    fresh = (
        mixed.reshape(count, KV_HEADS, group, HEAD_DIM),
        maxima.reshape(count, KV_HEADS, group),
        totals.reshape(count, KV_HEADS, group),
    )
    held_mixed, held_maxima, held_totals = tuple((made for made in fresh))
    back_mixed, back_maxima, back_totals = (
        lax.all_to_all(held_mixed, "ctx", split_axis=0, concat_axis=0, tiled=True),
        lax.all_to_all(held_maxima, "ctx", split_axis=0, concat_axis=0, tiled=True),
        lax.all_to_all(held_totals, "ctx", split_axis=0, concat_axis=0, tiled=True),
    )
    prefix_state = merge_parts(back_mixed, back_maxima, back_totals, ctx_size, rollouts, group)

    def climb(turn_index, carry):
        current, member = carry
        matched = current[:, None] == node_ids[None, :]
        member = member | matched
        lifted = jnp.sum(jnp.where(matched, parent[None, :], 0), axis=1)
        current = jnp.where(current >= 0, lifted, -1)
        return (current, member)

    start_member = jnp.zeros((leaf.shape[0], node_count), dtype=bool)
    ignored, member = lax.fori_loop(0, node_count, climb, (leaf, start_member))
    shard_piece = lax.all_gather(node_kv, "branch", axis=1, tiled=True)
    count = shard_piece.shape[1]
    live_mask = (member[:, :, None] & (token_ids[None, :] < node_len[:, None])[None, :, :]).reshape(
        member.shape[0], count * NODE_LEN
    )
    key_rows = shard_piece[0].reshape(count * NODE_LEN, KV_HEADS, HEAD_DIM)
    value_rows = shard_piece[1].reshape(count * NODE_LEN, KV_HEADS, HEAD_DIM)
    node_state = combine(
        (
            jnp.zeros((rollouts, KV_HEADS, group, HEAD_DIM), jnp.float32),
            jnp.full((rollouts, KV_HEADS, group), -jnp.inf, jnp.float32),
            jnp.zeros((rollouts, KV_HEADS, group), jnp.float32),
        ),
        attend(query_heads, key_rows, value_rows, live_mask),
    )
    front_state = combine(prefix_state, node_state)
    suffix_keys = suffix_kv[0].reshape(rollouts, -1, KV_HEADS, HEAD_DIM)
    suffix_values = suffix_kv[1].reshape(rollouts, -1, KV_HEADS, HEAD_DIM)
    suffix_scores = (
        jnp.einsum("rhgd,rshd->rhgs", query_heads, suffix_keys, preferred_element_type=jnp.float32)
        * inverse_root
    )
    positions = jnp.arange(suffix_keys.shape[1], dtype=jnp.int32)
    suffix_live = positions[None, :] < suffix_len[:, None]
    suffix_scores = jnp.where(suffix_live[:, None, None, :], suffix_scores, -jnp.inf)
    suffix_peak = jnp.max(suffix_scores, axis=-1)
    suffix_weights = jnp.exp(suffix_scores - suffix_peak[..., None])
    suffix_mixed = jnp.einsum(
        "rhgs,rshd->rhgd",
        suffix_weights.astype(jnp.bfloat16),
        suffix_values,
        preferred_element_type=jnp.float32,
    )
    suffix_state = (suffix_mixed, suffix_peak, jnp.sum(suffix_weights, axis=-1))
    fresh_keys = new_kv[0].reshape(rollouts, KV_HEADS, HEAD_DIM)
    fresh_values = new_kv[1].reshape(rollouts, KV_HEADS, HEAD_DIM).astype(jnp.float32)
    fresh_scores = (
        jnp.einsum("rhgd,rhd->rhg", query_heads, fresh_keys, preferred_element_type=jnp.float32)
        * inverse_root
    )
    fresh_mixed = jnp.broadcast_to(
        fresh_values[:, :, None, :], (rollouts, KV_HEADS, group, HEAD_DIM)
    )
    fresh_state = (fresh_mixed, fresh_scores, jnp.ones_like(fresh_scores))
    state = combine(combine(front_state, suffix_state), fresh_state)
    context = state[0] / state[2][..., None]
    return context.astype(jnp.bfloat16).reshape(rollouts, HEADS * HEAD_DIM)


def solution(mesh):
    return jax.shard_map(
        on_device,
        mesh=mesh,
        in_specs=(
            P(None, ("parts", "ctx"), None),
            P(("parts", "ctx", "branch"), None),
            P(None, ("parts", "ctx", "branch"), None),
            P(None, ("parts", "ctx", "branch"), None, None),
            P(("parts", "ctx", "branch")),
            P(None, ("parts", "branch"), None, None),
            P("parts"),
            P("parts"),
            P(("parts", "ctx", "branch")),
        ),
        out_specs=P(("parts", "ctx", "branch"), None),
        check_vma=False,
    )
```

profile of v0, /device:TPU:0, one launch (start us, length us, event | category | flops | bytes accessed | tf_op | source)
XLA Modules:
  0.0 144.7 jit_solution(16751887422370051576)
XLA Ops:
  8.0 4.0 %fusion.64 = (bf16[1,1024,1024]{2,1,0:T(8,128)(2,1)}, bf16[1,1024,1024]{2,1,0:T(8,128)(2,1)S(1)}) fusion(bf16[2,1024,1024]{2,1,0:T(8,128)(2,1)} %param.13), kind=kLoop, calls=%fused_computation.78 | loop fusion | bytes 8388608 | tf_op jit(solution)/shard_map/slice | solution.py:61
  12.0 2.6 %copy.184 = bf16[1,1024,1024]{1,2,0:T(8,128)(2,1)} copy(bf16[1,1024,1024]{2,1,0:T(8,128)(2,1)S(1)} %get-tuple-element.163) | data formatting | bytes 4194304
  14.6 3.0 %copy.125 = bf16[1024,8,128]{2,0,1:T(8,128)(2,1)S(1)} copy(bf16[1024,8,128]{0,2,1:T(8,128)(2,1)} %bitcast.128) | data formatting | bytes 4194304 | tf_op jit(solution)/shard_map/while | solution.py:74
  17.6 4.0 %copy.185 = bf16[1,1024,1024]{1,2,0:T(8,128)(2,1)} copy(bf16[1,1024,1024]{2,1,0:T(8,128)(2,1)} %get-tuple-element.162) | data formatting | bytes 4194304
  21.6 3.9 %copy.126 = bf16[1024,8,128]{2,0,1:T(8,128)(2,1)} copy(bf16[1024,8,128]{0,2,1:T(8,128)(2,1)} %bitcast.129) | data formatting | bytes 4194304 | tf_op jit(solution)/shard_map/while | solution.py:74
  26.0 13.6 %all-gather.3.cloned.1.call-done = bf16[64,8192]{1,0:T(8,128)(2,1)} async-done(((bf16[16,8192]{1,0:T(8,128)(2,1)}), bf16[64,8192]{1,0:T(8,128)(2,1)}) %all-gather.3.cloned.1.call-update) | async-done | bytes 1048592 | tf_op jit(solution)/shard_map/all_gather | solution.py:66
  39.6 1.5 %copy.190 = bf16[8,8,64,128]{3,2,1,0:T(8,128)(2,1)S(1)} copy(bf16[8,8,64,128]{3,1,2,0:T(8,128)(2,1)} %bitcast.141) | data formatting | bytes 2097152
  41.1 17.2 %while.27 = (s32[]{:T(128)}, f32[4,16,8,8,128]{4,3,2,1,0:T(8,128)}, f32[4,16,8,8]{3,2,1,0:T(8,128)S(1)}, f32[4,16,8,8]{3,2,1,0:T(8,128)}, bf16[4,16,8,8,128]{4,3...) while((s32[]{:T(128)}, f32[4,16,8,8,128]{4,3,2,1,0:T(8,128)}, ...), condition=%wide.region_3.4_spmd, body=%wide.region_0.3_spmd.sunk | while | flops 545259520 | bytes 27288692 | solution.py:74
  41.1 0.8 bitcast_reduce_fusion.2
  41.9 0.9 fusion.81
  43.5 1.0 fusion.80
  44.5 0.9 copy_dynamic-update-slice_fusion.5
  45.4 0.8 bitcast_reduce_fusion.2
  46.2 0.9 fusion.81
  47.9 1.0 fusion.80
  48.9 0.9 copy_dynamic-update-slice_fusion.5
  49.8 0.8 bitcast_reduce_fusion.2
  50.6 0.9 fusion.81
  52.2 1.0 fusion.80
  53.2 0.8 copy_dynamic-update-slice_fusion.5
  54.0 0.8 bitcast_reduce_fusion.2
  54.8 0.9 fusion.81
  56.4 1.0 fusion.80
  57.4 0.9 copy_dynamic-update-slice_fusion.5
  59.1 3.3 %all-to-all-start.1 = ((f32[4,1,1024]{2,1,0:T(1,128)}), f32[4,1,1024]{2,1,0:T(1,128)S(1)}, u32[]{:S(2)}, u32[]{:S(2)}) async-start(f32[4,1,1024]{2,1,0:T(1,128)} %reshape.165), calls=%async_computation.1 | async-start | bytes 32768 | tf_op jit(solution)/shard_map/all_to_all | solution.py:83
  62.4 5.0 %fusion.63 = (bf16[1,16,64,1024]{3,2,1,0:T(8,128)(2,1)}, bf16[1,16,64,1024]{3,2,1,0:T(8,128)(2,1)}) fusion(bf16[2,16,64,1024]{3,2,1,0:T(8,128)(2,1)} %param.16), kind=kLoop, calls=%fused_computation.77 | loop fusion | bytes 8388608 | tf_op jit(solution)/shard_map/slice | solution.py:115
  68.1 5.0 %all-to-all-start.2 = ((f32[4,1,1024]{2,1,0:T(1,128)}), f32[4,1,1024]{2,1,0:T(1,128)S(1)}, u32[]{:S(2)}, u32[]{:S(2)}) async-start(f32[4,1,1024]{2,1,0:T(1,128)} %reshape.167), calls=%async_computation.2 | async-start | bytes 32768 | tf_op jit(solution)/shard_map/all_to_all | solution.py:84
  73.3 2.2 %copy.195 = bf16[128,8,8,128]{3,2,1,0:T(8,128)(2,1)S(1)} copy(bf16[128,8,8,128]{3,1,2,0:T(8,128)(2,1)} %bitcast.131) | data formatting | bytes 4194304
  75.6 3.5 %copy.196 = bf16[128,8,8,128]{3,2,1,0:T(8,128)(2,1)} copy(bf16[128,8,8,128]{3,1,2,0:T(8,128)(2,1)} %bitcast.130) | data formatting | bytes 4194304
  79.8 5.2 %all-to-all-start = ((f32[64,8,8,128]{3,2,1,0:T(8,128)}), f32[64,8,8,128]{3,2,1,0:T(8,128)}, u32[]{:S(2)}, u32[]{:S(2)}) async-start(f32[64,8,8,128]{3,2,1,0:T(8,128)} %bitcast.12), calls=%async_computation | async-start | bytes 4194304 | tf_op jit(solution)/shard_map/all_to_all | solution.py:82
  85.3 0.9 fusion.68
  86.2 1.3 fusion.67
  87.4 1.6 %fusion.60 = (bf16[16,8,8,64]{3,2,1,0:T(8,128)(2,1)}, f32[16,8,8]{2,1,0:T(8,128)}) fusion(f32[16,8,8,64]{3,2,1,0:T(8,128)S(1)} %get-tuple-element.179, f32[16,8,8]{2,1,0:T(8,128)S(1)} %get-tuple-element.178), kind=kLoop, calls=%fused_computation.54 | loop fusion | flops 195584 | bytes 401408 | tf_op jit(solution)/shard_map/convert_element_type | solution.py:127
  92.0 1.7 %fusion.65 = (bf16[1,4,128,1024]{3,2,1,0:T(8,128)(2,1)S(1)}, bf16[1,4,128,1024]{3,2,1,0:T(8,128)(2,1)S(1)}) fusion(bf16[2,4,128,1024]{3,2,1,0:T(8,128)(2,1)} %all-gather.5.cloned.1.call-done), kind=kLoop, calls=%fused_computation.79 | loop fusion | bytes 4194304 | tf_op jit(solution)/shard_map/slice | solution.py:103
  94.7 1.3 fusion.66
  96.0 1.5 %copy.133 = f32[16,8,8]{2,1,0:T(8,128)} copy(f32[16,8,8]{0,2,1:T(8,128)} %get-tuple-element.176) | data formatting | bytes 8192 | tf_op jit(solution)/shard_map/reduce_max | solution.py:18
  97.5 1.6 %exponential_multiply_fusion = (f32[16,8,8]{2,1,0:T(8,128)}, f32[16,8,8]{2,1,0:T(8,128)}, f32[16,8,8]{2,1,0:T(8,128)}, f32[16,8,8]{2,1,0:T(8,128)}) fusion(f32[16,8,8]{2,1,0:T(8,128)} %copy.133, f32[16,8,8]{2,1,0:T(8,128)S(1)} %reduce_max.36), kind=kLoop, calls=%fused_computation.72 | loop fusion | flops 6144 | bytes 24576 | tf_op jit(solution)/shard_map/mul;broadcast_in_dim | solution.py:38
  99.0 1.5 %copy.139 = f32[16,8,8]{0,2,1:T(8,128)} copy(f32[16,8,8]{2,1,0:T(8,128)} %get-tuple-element.174) | data formatting | bytes 8192 | tf_op jit(solution)/shard_map/jit(_where)/select_n | solution.py:35
  100.6 2.7 %fusion.25 = (f32[16,8,8]{0,2,1:T(8,128)}, bf16[16,8,8,512]{3,0,2,1:T(8,128)(2,1)}) fusion(f32[16,8,8,512]{3,0,2,1:T(8,128)S(1)} %get-tuple-element.177, f32[16,8,8]{0,2,1:T(8,128)} %copy.139), kind=kLoop, calls=%fused_computation.32 | loop fusion | flops 1571840 | bytes 3153920 | tf_op jit(solution)/shard_map/reduce_sum | solution.py:21
  103.3 0.8 copy.156
  104.1 1.1 multiply_add_fusion
  105.3 0.9 copy.138
  106.1 0.9 copy.143
  107.4 25.0 %all-to-all-done = f32[64,8,8,128]{3,2,1,0:T(8,128)} async-done(((f32[64,8,8,128]{3,2,1,0:T(8,128)}), f32[64,8,8,128]{3,2,1,0:T(8,128)}, u32[]{:S(2)}, u32[]{:S(2)}) %all-to-all-start) | async-done | bytes 2097184 | tf_op jit(solution)/shard_map/all_to_all | solution.py:82
  132.4 2.0 %multiply_reduce_fusion = f32[16,8,8,128]{3,2,1,0:T(8,128)S(1)} fusion(f32[4,16,8,8,128]{4,3,2,1,0:T(8,128)} %bitcast.13, f32[4,16,8,8]{3,2,1,0:T(8,128)S(1)} %subtract_exponential_fusion.2), kind=kLoop, calls=%fused_computation.31 | loop fusion | flops 917504 | bytes 2637824 | tf_op jit(solution)/shard_map/reduce_sum | solution.py:49
  134.4 1.5 %fusion.52 = f32[16,8,8,128]{3,2,0,1:T(8,128)S(1)} fusion(bf16[512,8,128,1]{2,1,0,3:T(8,128)(2,1)S(1)} %bitcast.142, bf16[16,8,8,512]{3,0,2,1:T(8,128)(2,1)S(1)} %copy-done.2, f32[16,8,8,128]{3,2,1,0:T(8,128)S(1)} %multiply_reduce_fusion, f32[16,8,8]{2,0,1:T(8,128)S(1)} %copy.147, f32[16,8,8]{2,0,1:T(8,128)S(1)} %copy.145, f32[16,8,8]{2,0,1:T(8,128)S(1)} %copy.143, ...), kind=kOutput, calls=%fused_computation.46 | convolution fusion | flops 135004160 | bytes 3166208 | tf_op jit(solution)/shard_map/bhgt,thd->bhgd/dot_general | solution.py:22
  136.0 1.0 fusion.53
  137.0 0.9 copy.247
  (97 shorter events, 12.4 us)
Async XLA Ops:
  6.5 33.1 %all-gather.3.cloned.1.call-start = ((), (), s32[]{:S(2)}) async-start(), calls=%async_computation.3 | async-start | bytes 1310720 | tf_op jit(solution)/shard_map/all_gather | solution.py:66
  7.3 84.8 %all-gather.5.cloned.1.call-start = ((), (), s32[]{:S(2)}) async-start(), calls=%async_computation.4 | async-start | bytes 2621440 | tf_op jit(solution)/shard_map/all_gather | solution.py:98
  21.6 3.9 %copy-start.10 = (s32[16]{0:T(128)S(1)}, s32[16]{0:T(128)}, u32[]{:S(2)}) copy-start(s32[16]{0:T(128)} %param.21) | copy-start | bytes 196
  21.6 3.9 %copy-start.13 = (s32[4]{0:T(128)S(1)}, s32[4]{0:T(128)}, u32[]{:S(2)}) copy-start(s32[4]{0:T(128)} %param.20) | copy-start | bytes 52
  41.9 1.6 %copy-start = (bf16[1024,8,128]{2,0,1:T(8,128)(2,1)S(1)}, bf16[1024,8,128]{2,0,1:T(8,128)(2,1)}, u32[]{:S(2)}) copy-start(bf16[1024,8,128]{2,0,1:T(8,128)(2,1)} %get-tuple-element.296) | copy-start | bytes 6291460 | tf_op jit(solution)/shard_map/while
  46.2 1.7 %copy-start = (bf16[1024,8,128]{2,0,1:T(8,128)(2,1)S(1)}, bf16[1024,8,128]{2,0,1:T(8,128)(2,1)}, u32[]{:S(2)}) copy-start(bf16[1024,8,128]{2,0,1:T(8,128)(2,1)} %get-tuple-element.296) | copy-start | bytes 6291460 | tf_op jit(solution)/shard_map/while
  50.6 1.6 %copy-start = (bf16[1024,8,128]{2,0,1:T(8,128)(2,1)S(1)}, bf16[1024,8,128]{2,0,1:T(8,128)(2,1)}, u32[]{:S(2)}) copy-start(bf16[1024,8,128]{2,0,1:T(8,128)(2,1)} %get-tuple-element.296) | copy-start | bytes 6291460 | tf_op jit(solution)/shard_map/while
  54.8 1.6 %copy-start = (bf16[1024,8,128]{2,0,1:T(8,128)(2,1)S(1)}, bf16[1024,8,128]{2,0,1:T(8,128)(2,1)}, u32[]{:S(2)}) copy-start(bf16[1024,8,128]{2,0,1:T(8,128)(2,1)} %get-tuple-element.296) | copy-start | bytes 6291460 | tf_op jit(solution)/shard_map/while
  59.1 9.0 %all-to-all-start.1 = ((f32[4,1,1024]{2,1,0:T(1,128)}), f32[4,1,1024]{2,1,0:T(1,128)S(1)}, u32[]{:S(2)}, u32[]{:S(2)}) async-start(f32[4,1,1024]{2,1,0:T(1,128)} %reshape.165), calls=%async_computation.1 | async-start | bytes 32768 | tf_op jit(solution)/shard_map/all_to_all | solution.py:83
  62.3 5.0 %copy-start.7 = (f32[4,16,8,8]{3,2,1,0:T(8,128)S(1)}, f32[4,16,8,8]{3,2,1,0:T(8,128)}, u32[]{:S(2)}) copy-start(f32[4,16,8,8]{3,2,1,0:T(8,128)} %get-tuple-element.74) | copy-start | bytes 49156
  62.3 10.8 %copy-start.8 = (bf16[2,16,1024]{2,1,0:T(8,128)(2,1)S(1)}, bf16[2,16,1024]{2,1,0:T(8,128)(2,1)}, u32[]{:S(2)}) copy-start(bf16[2,16,1024]{2,1,0:T(8,128)(2,1)} %param.15) | copy-start | bytes 196612
  62.4 10.8 %copy-start.5 = (bf16[16,8192]{1,0:T(8,128)(2,1)S(1)}, bf16[16,8192]{1,0:T(8,128)(2,1)}, u32[]{:S(2)}) copy-start(bf16[16,8192]{1,0:T(8,128)(2,1)} %param.14) | copy-start | bytes 786436
  68.1 11.6 %all-to-all-start.2 = ((f32[4,1,1024]{2,1,0:T(1,128)}), f32[4,1,1024]{2,1,0:T(1,128)S(1)}, u32[]{:S(2)}, u32[]{:S(2)}) async-start(f32[4,1,1024]{2,1,0:T(1,128)} %reshape.167), calls=%async_computation.2 | async-start | bytes 32768 | tf_op jit(solution)/shard_map/all_to_all | solution.py:84
  73.2 13.0 %copy-start.3 = (bf16[2,8,64,128]{3,2,1,0:T(8,128)(2,1)}, bf16[2,8,64,128]{3,2,1,0:T(8,128)(2,1)S(1)}, u32[]{:S(2)}) copy-start(bf16[2,8,64,128]{3,2,1,0:T(8,128)(2,1)S(1)} %copy.193) | copy-start | bytes 786436
  79.8 5.2 %copy-start.11 = (s32[4]{0:T(128)S(1)}, s32[4]{0:T(128)}, u32[]{:S(2)}) copy-start(s32[4]{0:T(128)} %param.19) | copy-start | bytes 52
  79.8 5.3 %copy-start.12 = (s32[16]{0:T(128)S(1)}, s32[16]{0:T(128)}, u32[]{:S(2)}) copy-start(s32[16]{0:T(128)} %param.17) | copy-start | bytes 196
  79.8 52.6 %all-to-all-start = ((f32[64,8,8,128]{3,2,1,0:T(8,128)}), f32[64,8,8,128]{3,2,1,0:T(8,128)}, u32[]{:S(2)}, u32[]{:S(2)}) async-start(f32[64,8,8,128]{3,2,1,0:T(8,128)} %bitcast.12), calls=%async_computation | async-start | bytes 4194304 | tf_op jit(solution)/shard_map/all_to_all | solution.py:82
  93.7 1.0 copy-start.4
  107.3 27.1 %copy-start.2 = (bf16[16,8,8,512]{3,0,2,1:T(8,128)(2,1)S(1)}, bf16[16,8,8,512]{3,0,2,1:T(8,128)(2,1)}, u32[]{:S(2)}) copy-start(bf16[16,8,8,512]{3,0,2,1:T(8,128)(2,1)} %get-tuple-element.165) | copy-start | bytes 3145732
  134.4 1.6 %copy-start.1 = (bf16[128,8,8,128]{3,2,1,0:T(8,128)(2,1)S(1)}, bf16[128,8,8,128]{3,2,1,0:T(8,128)(2,1)}, u32[]{:S(2)}) copy-start(bf16[128,8,8,128]{3,2,1,0:T(8,128)(2,1)} %copy.196) | copy-start | bytes 6291460
  134.4 1.6 %copy-start.6 = (bf16[16,8,8,64]{3,2,1,0:T(8,128)(2,1)S(1)}, bf16[16,8,8,64]{3,2,1,0:T(8,128)(2,1)}, u32[]{:S(2)}) copy-start(bf16[16,8,8,64]{3,2,1,0:T(8,128)(2,1)} %get-tuple-element.168) | copy-start | bytes 393220
  134.4 1.6 %copy-start.9 = (f32[16,8,128]{2,0,1:T(8,128)S(1)}, f32[16,8,128]{2,0,1:T(8,128)}, u32[]{:S(2)}) copy-start(f32[16,8,128]{2,0,1:T(8,128)} %copy.152) | copy-start | bytes 196612
Sparse Core Ops, SparseCore 0:
  8.9 30.6 all-gather.2
  41.2 22.0 all-gather.4
where the time goes:
time: 146 us; the launch traced here: 145 us
  local copies, waits for them, and re-layouts  49.2 us (34%)
  waiting for transfers between devices  40 us (27%)
  other arithmetic  15 us (10%)
  between operations  13.8 us (9%)
  starting transfers between devices  13.5 us (9%)
  matrix products  13.1 us (9%)
    all_to_all x1, waiting for transfers between devices, on_device(): lax.all_to_all(held_mixed, 'ctx', split_axis=0, concat_axis=0, tiled=True)  25 us
    unnamed x40, local copies, waits for them, and re-layouts  17.8 us
    all_gather x1, waiting for transfers between devices, on_device(): query_rows = lax.all_gather(queries, 'ctx', axis=0, tiled=True)  13.6 us
    while x2, local copies, waits for them, and re-layouts, on_device(): mixed, maxima, totals = lax.map(one_block, blocks)  6.96 us
    dynamic_update_slice x8, local copies, waits for them, and re-layouts, on_device(): mixed, maxima, totals = lax.map(one_block, blocks)  6.15 us
    reduce_sum x5, other arithmetic, attend(): totals = jnp.sum(weights, axis=-1)  6.14 us
    dot_general x5, matrix products, attend(): jnp.einsum('bhgt,thd->bhgd', weights.astype(jnp.bfloat16), value_rows, pr...  5.48 us
    all_to_all x1, starting transfers between devices, on_device(): lax.all_to_all(held_mixed, 'ctx', split_axis=0, concat_axis=0, tiled=True)  5.22 us
  transfers between devices with their start and end apart: 5, of which 2 were waited for; matrix products, arithmetic and copies ran while one was open for 49% of the time, Pallas kernels for 0%

commit v1 on v0

--- a/solution.py
+++ b/solution.py
@@ -8,6 +8,28 @@
 KV_HEADS = 8
 HEAD_DIM = 128
 NODE_LEN = 128
+
+
+def cut_along(array, dim, size):
+    before, after = (array.shape[:dim], array.shape[dim + 1 :])
+    return jnp.moveaxis(array.reshape(*before, size, -1, *after), dim, 0)
+
+
+def laid_out(parts, dim):
+    shape = list(parts.shape[1:])
+    shape[dim] *= parts.shape[0]
+    return jnp.moveaxis(parts, 0, dim).reshape(shape)
+
+
+def pairwise_exchange(shard, axis, split_dim, concat_dim):
+    size, index = (lax.axis_size(axis), lax.axis_index(axis))
+    tiles = cut_along(shard, split_dim, size)
+    outs = [tiles[index]]
+    for step in range(1, size):
+        sent = tiles[index ^ step]
+        outs.append(lax.ppermute(sent, axis, [(i, i ^ step) for i in range(size)]))
+    tiles = jnp.stack(outs)[index ^ jnp.arange(size)]
+    return laid_out(tiles, concat_dim)
 
 
 def attend(query_block, key_rows, value_rows, live_mask):
@@ -81,7 +103,7 @@
     back_mixed, back_maxima, back_totals = (
         lax.all_to_all(held_mixed, "ctx", split_axis=0, concat_axis=0, tiled=True),
         lax.all_to_all(held_maxima, "ctx", split_axis=0, concat_axis=0, tiled=True),
-        lax.all_to_all(held_totals, "ctx", split_axis=0, concat_axis=0, tiled=True),
+        pairwise_exchange(held_totals, "ctx", 0, 0),
     )
     prefix_state = merge_parts(back_mixed, back_maxima, back_totals, ctx_size, rollouts, group)
 

time: 146 us -> 158 us (1.082)
  local copies, waits for them, and re-layouts: 49.2 us -> 61.3 us
  waiting for transfers between devices: 40 us -> 48.1 us
  other arithmetic: 15 us -> 8.62 us
  starting transfers between devices: 13.5 us -> 11.6 us
    ppermute x0 -> x3, waiting for transfers between devices: none -> 36.7 us  [pairwise_exchange(): outs.append(lax.ppermute(sent, axis, [(i, i ^ step) for i in range(size)]))]
    all_to_all x1, waiting for transfers between devices: 25 us -> 0.01 us  [on_device(): lax.all_to_all(held_mixed, 'ctx', split_axis=0, concat_axis=0, tiled=True)]
    all_gather x1, waiting for transfers between devices: 13.6 us -> 7.2 us  [on_device(): query_rows = lax.all_gather(queries, 'ctx', axis=0, tiled=True)]
    all_to_all x1 -> x0, starting transfers between devices: 5.03 us -> none  [on_device(): lax.all_to_all(held_totals, 'ctx', split_axis=0, concat_axis=0, tiled=True)]
    ppermute x0 -> x3, starting transfers between devices: none -> 4.42 us  [pairwise_exchange(): outs.append(lax.ppermute(sent, axis, [(i, i ^ step) for i in range(size)]))]
    exp x3, local copies, waits for them, and re-layouts: 0.04 us -> 3.62 us  [combine(): scale_a = jnp.exp(maxima_a - anchor)]
    while x8, local copies, waits for them, and re-layouts: 0.36 us -> 3.3 us
    all_to_all x1, waiting for transfers between devices: 0.01 us -> 2.72 us  [on_device(): lax.all_to_all(held_maxima, 'ctx', split_axis=0, concat_axis=0, tiled=True)]
  transfers between devices with their start and end apart: 5 -> 7, of which waited for: 2 -> 4; matrix products, arithmetic and copies ran while one was open for 49% -> 48% of each run, Pallas kernels for 0% -> 0%
where the time goes in v1:
time: 158 us; the launch traced here: 157 us
  local copies, waits for them, and re-layouts  61.3 us (39%)
  waiting for transfers between devices  48.1 us (30%)
  between operations  13.9 us (9%)
  matrix products  13.5 us (9%)
  starting transfers between devices  11.6 us (7%)
  other arithmetic  8.62 us (5%)
    ppermute x3, waiting for transfers between devices, pairwise_exchange(): outs.append(lax.ppermute(sent, axis, [(i, i ^ step) for i in range(size)]))  36.7 us
    unnamed x71, local copies, waits for them, and re-layouts  18.6 us
    dynamic_update_slice x12, local copies, waits for them, and re-layouts, on_device(): mixed, maxima, totals = lax.map(one_block, blocks)  8.61 us
    all_gather x1, waiting for transfers between devices, on_device(): query_rows = lax.all_gather(queries, 'ctx', axis=0, tiled=True)  7.2 us
    while x3, local copies, waits for them, and re-layouts, on_device(): mixed, maxima, totals = lax.map(one_block, blocks)  7.08 us
    dot_general x5, matrix products, attend(): jnp.einsum('bhgt,thd->bhgd', weights.astype(jnp.bfloat16), value_rows, pr...  5.49 us
    reduce_sum x5, other arithmetic, attend(): totals = jnp.sum(weights, axis=-1)  4.83 us
    ppermute x3, starting transfers between devices, pairwise_exchange(): outs.append(lax.ppermute(sent, axis, [(i, i ^ step) for i in range(size)]))  4.42 us
  transfers between devices with their start and end apart: 7, of which 4 were waited for; matrix products, arithmetic and copies ran while one was open for 48% of the time, Pallas kernels for 0%

profile of v1, /device:TPU:0, one launch (start us, length us, event | category | flops | bytes accessed | tf_op | source)
XLA Modules:
  0.0 157.1 jit_solution(14423607416140186390)
XLA Ops:
  8.0 4.0 %fusion.65 = (bf16[1,1024,1024]{2,1,0:T(8,128)(2,1)}, bf16[1,1024,1024]{2,1,0:T(8,128)(2,1)S(1)}) fusion(bf16[2,1024,1024]{2,1,0:T(8,128)(2,1)} %param.13), kind=kLoop, calls=%fused_computation.88 | loop fusion | bytes 8388608 | tf_op jit(solution)/shard_map/slice | solution.py:83
  12.0 2.6 %copy.185 = bf16[1,1024,1024]{1,2,0:T(8,128)(2,1)} copy(bf16[1,1024,1024]{2,1,0:T(8,128)(2,1)S(1)} %get-tuple-element.163) | data formatting | bytes 4194304
  14.6 3.0 %copy.126 = bf16[1024,8,128]{2,0,1:T(8,128)(2,1)S(1)} copy(bf16[1024,8,128]{0,2,1:T(8,128)(2,1)} %bitcast.141) | data formatting | bytes 4194304 | tf_op jit(solution)/shard_map/while | solution.py:96
  17.6 4.0 %copy.186 = bf16[1,1024,1024]{1,2,0:T(8,128)(2,1)} copy(bf16[1,1024,1024]{2,1,0:T(8,128)(2,1)} %get-tuple-element.162) | data formatting | bytes 4194304
  21.6 3.9 %copy.127 = bf16[1024,8,128]{2,0,1:T(8,128)(2,1)} copy(bf16[1024,8,128]{0,2,1:T(8,128)(2,1)} %bitcast.142) | data formatting | bytes 4194304 | tf_op jit(solution)/shard_map/while | solution.py:96
  26.1 4.2 %fusion.64 = (bf16[1,16,64,1024]{3,2,1,0:T(8,128)(2,1)}, bf16[1,16,64,1024]{3,2,1,0:T(8,128)(2,1)S(1)}) fusion(bf16[2,16,64,1024]{3,2,1,0:T(8,128)(2,1)} %param.16), kind=kLoop, calls=%fused_computation.87 | loop fusion | bytes 8388608 | tf_op jit(solution)/shard_map/slice | solution.py:137
  30.3 2.0 %copy.196 = bf16[128,8,8,128]{3,2,1,0:T(8,128)(2,1)} copy(bf16[128,8,8,128]{3,1,2,0:T(8,128)(2,1)S(1)} %bitcast.144) | data formatting | bytes 4194304
  32.4 7.2 %all-gather.3.cloned.1.call-done = bf16[64,8192]{1,0:T(8,128)(2,1)} async-done(((bf16[16,8192]{1,0:T(8,128)(2,1)}), bf16[64,8192]{1,0:T(8,128)(2,1)}) %all-gather.3.cloned.1.call-update) | async-done | bytes 1048592 | tf_op jit(solution)/shard_map/all_gather | solution.py:88
  39.6 1.5 copy.191
  41.1 22.6 %while.27 = (s32[]{:T(128)}, f32[4,16,8,8,128]{4,3,2,1,0:T(8,128)}, f32[4,16,8,8]{3,2,1,0:T(8,128)}, f32[4,16,8,8]{3,1,2,0:T(8,128)}, bf16[4,16,8,8,128]{4,3,2,1...) while((s32[]{:T(128)}, f32[4,16,8,8,128]{4,3,2,1,0:T(8,128)}, ...), condition=%wide.region_3.4_spmd, body=%wide.region_0.3_spmd.sunk | while | flops 545259520 | bytes 27166324 | solution.py:96
  41.1 0.8 bitcast_reduce_fusion.2
  42.7 1.0 fusion.81
  43.7 0.9 copy_dynamic-update-slice_fusion.4
  44.6 0.9 fusion.82
  47.6 0.9 copy-done
  48.5 1.0 fusion.81
  49.5 0.9 copy_dynamic-update-slice_fusion.4
  50.3 0.9 fusion.82
  52.5 0.8 bitcast_reduce_fusion.2
  53.3 0.8 copy-done
  54.1 1.0 fusion.81
  55.1 0.9 copy_dynamic-update-slice_fusion.4
  55.9 0.9 fusion.82
  58.9 0.8 copy-done
  59.7 1.0 fusion.81
  60.7 0.9 copy_dynamic-update-slice_fusion.4
  61.6 0.9 fusion.82
  63.7 1.7 %reshape.181 = f32[4,1,1024]{2,1,0:T(1,128)} reshape(f32[64,8,8]{2,1,0:T(8,128)} %bitcast.14) | data formatting | bytes 32768
  65.4 3.2 %all-to-all-start.1 = ((f32[4,1,1024]{2,1,0:T(1,128)}), f32[4,1,1024]{2,1,0:T(1,128)S(1)}, u32[]{:S(2)}, u32[]{:S(2)}) async-start(f32[4,1,1024]{2,1,0:T(1,128)} %reshape.181), calls=%async_computation.1 | async-start | bytes 32768 | tf_op jit(solution)/shard_map/all_to_all | solution.py:105
  68.6 2.9 %fusion.68 = (f32[16,8,8]{2,1,0:T(8,128)S(1)}, f32[16,8,8,64]{3,2,1,0:T(8,128)S(1)}) fusion(bf16[16,8,8,128]{3,2,1,0:T(8,128)(2,1)S(1)} %bitcast.152, bf16[16,64,8,128]{3,2,1,0:T(8,128)(2,1)} %bitcast.139, pred[16,64]{1,0:T(8,128)(4,1)S(1)} %iota_compare_fusion.1), kind=kOutput, calls=%fused_computation.91 | convolution fusion | flops 16972800 | bytes 2626560 | tf_op jit(solution)/shard_map/rhgd,rshd->rhgs/dot_general | solution.py:139
  71.5 2.7 %all-to-all-done.1 = f32[4,1,1024]{2,1,0:T(1,128)S(1)} async-done(((f32[4,1,1024]{2,1,0:T(1,128)}), f32[4,1,1024]{2,1,0:T(1,128)S(1)}, u32[]{:S(2)}, u32[]{:S(2)}) %all-to-all-start.1) | async-done | bytes 16416 | tf_op jit(solution)/shard_map/all_to_all | solution.py:105
  74.2 3.9 %all-to-all-start = ((f32[64,8,8,128]{3,2,1,0:T(8,128)}), f32[64,8,8,128]{3,2,1,0:T(8,128)S(1)}, u32[]{:S(2)}, u32[]{:S(2)}) async-start(f32[64,8,8,128]{3,2,1,0:T(8,128)} %bitcast.151), calls=%async_computation | async-start | bytes 4194304 | tf_op jit(solution)/shard_map/all_to_all | solution.py:104
  78.2 0.9 fusion.60
  81.6 3.6 %copy.197 = bf16[128,8,8,128]{3,2,1,0:T(8,128)(2,1)} copy(bf16[128,8,8,128]{3,1,2,0:T(8,128)(2,1)} %bitcast.143) | data formatting | bytes 4194304
  86.3 1.8 %collective-permute-start = (f32[16,8,8]{0,2,1:T(8,128)S(1)}, f32[16,8,8]{0,2,1:T(8,128)S(1)}, u32[]{:S(2)}, u32[]{:S(2)}) collective-permute-start(f32[16,8,8]{0,2,1:T(8,128)S(1)} %bitcast.161), channel_id=1, source_target_pairs={{0,4},{4,0},{8,12},{12,8},{1,5},{5,1},{9,13},{13,9},{2,6},{6,2},{1... | collective-permute-start | bytes 12296 | tf_op jit(solution)/shard_map/ppermute | solution.py:30
  88.2 2.4 %collective-permute-start.1 = (f32[16,8,8]{0,2,1:T(8,128)S(1)}, f32[16,8,8]{0,2,1:T(8,128)S(1)}, u32[]{:S(2)}, u32[]{:S(2)}) collective-permute-start(f32[16,8,8]{0,2,1:T(8,128)S(1)} %bitcast.162), channel_id=1, source_target_pairs={{0,8},{4,12},{8,0},{12,4},{1,9},{5,13},{9,1},{13,5},{2,10},{6,14},... | collective-permute-start | bytes 12296 | tf_op jit(solution)/shard_map/ppermute | solution.py:30
  90.8 21.6 %collective-permute-done = f32[16,8,8]{0,2,1:T(8,128)S(1)} collective-permute-done((f32[16,8,8]{0,2,1:T(8,128)S(1)}, f32[16,8,8]{0,2,1:T(8,128)S(1)}, u32[]{:S(2)}, u32[]{:S(2)}) %collective-permute-start) | collective-permute-done | bytes 4128 | tf_op jit(solution)/shard_map/ppermute | solution.py:30
  112.4 15.1 %collective-permute-done.1 = f32[16,8,8]{0,2,1:T(8,128)S(1)} collective-permute-done((f32[16,8,8]{0,2,1:T(8,128)S(1)}, f32[16,8,8]{0,2,1:T(8,128)S(1)}, u32[]{:S(2)}, u32[]{:S(2)}) %collective-permute-start.1) | collective-permute-done | bytes 4128 | tf_op jit(solution)/shard_map/ppermute | solution.py:30
  129.8 0.8 copy.133
  130.7 1.7 %fusion.66 = (bf16[1,4,128,1024]{3,2,1,0:T(8,128)(2,1)S(1)}, bf16[1,4,128,1024]{3,2,1,0:T(8,128)(2,1)S(1)}) fusion(bf16[2,4,128,1024]{3,2,1,0:T(8,128)(2,1)} %all-gather.5.cloned.1.call-done), kind=kLoop, calls=%fused_computation.89 | loop fusion | bytes 4194304 | tf_op jit(solution)/shard_map/slice | solution.py:125
  133.4 1.4 fusion.25
  135.6 1.5 copy.137
  137.0 1.5 copy.143
  138.5 1.5 copy.146
  141.3 1.2 copy.195
  146.7 1.5 fusion.52
  148.3 1.0 fusion.53
  149.4 0.9 copy.247
  (146 shorter events, 23.4 us)
Async XLA Ops:
  6.5 33.1 %all-gather.3.cloned.1.call-start = ((), (), s32[]{:S(2)}) async-start(), calls=%async_computation.2 | async-start | bytes 1310720 | tf_op jit(solution)/shard_map/all_gather | solution.py:88
  7.3 123.4 %all-gather.5.cloned.1.call-start = ((), (), s32[]{:S(2)}) async-start(), calls=%async_computation.3 | async-start | bytes 2621440 | tf_op jit(solution)/shard_map/all_gather | solution.py:120
  21.6 4.0 %copy-start.4 = (bf16[16,8192]{1,0:T(8,128)(2,1)S(1)}, bf16[16,8192]{1,0:T(8,128)(2,1)}, u32[]{:S(2)}) copy-start(bf16[16,8192]{1,0:T(8,128)(2,1)} %param.14) | copy-start | bytes 786436
  21.6 4.0 %copy-start.26 = (s32[16]{0:T(128)S(1)}, s32[16]{0:T(128)}, u32[]{:S(2)}) copy-start(s32[16]{0:T(128)} %param.21) | copy-start | bytes 196
  21.6 4.0 %copy-start.29 = (s32[4]{0:T(128)S(1)}, s32[4]{0:T(128)}, u32[]{:S(2)}) copy-start(s32[4]{0:T(128)} %param.20) | copy-start | bytes 52
  30.3 2.0 %copy-start.27 = (s32[16]{0:T(128)S(1)}, s32[16]{0:T(128)}, u32[]{:S(2)}) copy-start(s32[16]{0:T(128)} %param.17) | copy-start | bytes 196
  41.1 1.6 %copy-start = (bf16[1024,8,128]{2,0,1:T(8,128)(2,1)S(1)}, bf16[1024,8,128]{2,0,1:T(8,128)(2,1)}, u32[]{:S(2)}) copy-start(bf16[1024,8,128]{2,0,1:T(8,128)(2,1)} %get-tuple-element.295) | copy-start | bytes 6291460 | tf_op jit(solution)/shard_map/while
  46.7 1.7 %copy-start = (bf16[1024,8,128]{2,0,1:T(8,128)(2,1)S(1)}, bf16[1024,8,128]{2,0,1:T(8,128)(2,1)}, u32[]{:S(2)}) copy-start(bf16[1024,8,128]{2,0,1:T(8,128)(2,1)} %get-tuple-element.295) | copy-start | bytes 6291460 | tf_op jit(solution)/shard_map/while
  52.5 1.6 %copy-start = (bf16[1024,8,128]{2,0,1:T(8,128)(2,1)S(1)}, bf16[1024,8,128]{2,0,1:T(8,128)(2,1)}, u32[]{:S(2)}) copy-start(bf16[1024,8,128]{2,0,1:T(8,128)(2,1)} %get-tuple-element.295) | copy-start | bytes 6291460 | tf_op jit(solution)/shard_map/while
  58.1 1.6 %copy-start = (bf16[1024,8,128]{2,0,1:T(8,128)(2,1)S(1)}, bf16[1024,8,128]{2,0,1:T(8,128)(2,1)}, u32[]{:S(2)}) copy-start(bf16[1024,8,128]{2,0,1:T(8,128)(2,1)} %get-tuple-element.295) | copy-start | bytes 6291460 | tf_op jit(solution)/shard_map/while
  65.4 8.8 %all-to-all-start.1 = ((f32[4,1,1024]{2,1,0:T(1,128)}), f32[4,1,1024]{2,1,0:T(1,128)S(1)}, u32[]{:S(2)}, u32[]{:S(2)}) async-start(f32[4,1,1024]{2,1,0:T(1,128)} %reshape.181), calls=%async_computation.1 | async-start | bytes 32768 | tf_op jit(solution)/shard_map/all_to_all | solution.py:105
  74.2 6.3 %copy-start.24 = (bf16[2,16,1024]{2,1,0:T(8,128)(2,1)S(1)}, bf16[2,16,1024]{2,1,0:T(8,128)(2,1)}, u32[]{:S(2)}) copy-start(bf16[2,16,1024]{2,1,0:T(8,128)(2,1)} %param.15) | copy-start | bytes 196612
  74.2 71.2 %all-to-all-start = ((f32[64,8,8,128]{3,2,1,0:T(8,128)}), f32[64,8,8,128]{3,2,1,0:T(8,128)S(1)}, u32[]{:S(2)}, u32[]{:S(2)}) async-start(f32[64,8,8,128]{3,2,1,0:T(8,128)} %bitcast.151), calls=%async_computation | async-start | bytes 4194304 | tf_op jit(solution)/shard_map/all_to_all | solution.py:104
  81.6 4.2 %copy-start.28 = (s32[4]{0:T(128)S(1)}, s32[4]{0:T(128)}, u32[]{:S(2)}) copy-start(s32[4]{0:T(128)} %param.19) | copy-start | bytes 52
  81.6 4.4 %copy-start.6 = (f32[4,16,8,8]{3,1,2,0:T(8,128)S(1)}, f32[4,16,8,8]{3,1,2,0:T(8,128)}, u32[]{:S(2)}) copy-start(f32[4,16,8,8]{3,1,2,0:T(8,128)} %get-tuple-element.74) | copy-start | bytes 49156
  86.3 26.2 %collective-permute-start = (f32[16,8,8]{0,2,1:T(8,128)S(1)}, f32[16,8,8]{0,2,1:T(8,128)S(1)}, u32[]{:S(2)}, u32[]{:S(2)}) collective-permute-start(f32[16,8,8]{0,2,1:T(8,128)S(1)} %bitcast.161), channel_id=1, source_target_pairs={{0,4},{4,0},{8,12},{12,8},{1,5},{5,1},{9,13},{13,9},{2,6},{6,2},{1... | collective-permute-start | bytes 12296 | tf_op jit(solution)/shard_map/ppermute | solution.py:30
  88.2 39.4 %collective-permute-start.1 = (f32[16,8,8]{0,2,1:T(8,128)S(1)}, f32[16,8,8]{0,2,1:T(8,128)S(1)}, u32[]{:S(2)}, u32[]{:S(2)}) collective-permute-start(f32[16,8,8]{0,2,1:T(8,128)S(1)} %bitcast.162), channel_id=1, source_target_pairs={{0,8},{4,12},{8,0},{12,4},{1,9},{5,13},{9,1},{13,5},{2,10},{6,14},... | collective-permute-start | bytes 12296 | tf_op jit(solution)/shard_map/ppermute | solution.py:30
  90.6 37.0 %collective-permute-start.2 = (f32[16,8,8]{0,2,1:T(8,128)S(1)}, f32[16,8,8]{0,2,1:T(8,128)S(1)}, u32[]{:S(2)}, u32[]{:S(2)}) collective-permute-start(f32[16,8,8]{0,2,1:T(8,128)S(1)} %bitcast.163), channel_id=1, source_target_pairs={{0,12},{4,8},{8,4},{12,0},{1,13},{5,9},{9,5},{13,1},{2,14},{6,10},... | collective-permute-start | bytes 12296 | tf_op jit(solution)/shard_map/ppermute | solution.py:30
  133.4 1.5 copy-start.8
  133.4 1.4 copy-start.9
  133.4 1.4 copy-start.10
  134.8 10.6 %copy-start.5 = (f32[4,16,8,8]{3,2,1,0:T(8,128)S(1)}, f32[4,16,8,8]{3,2,1,0:T(8,128)}, u32[]{:S(2)}) copy-start(f32[4,16,8,8]{3,2,1,0:T(8,128)} %copy.133) | copy-start | bytes 49156
  135.6 8.5 %copy-start.12 = (f32[16,8,8]{0,2,1:T(8,128)S(1)}, f32[16,8,8]{0,2,1:T(8,128)}, u32[]{:S(2)}) copy-start(f32[16,8,8]{0,2,1:T(8,128)} %get-tuple-element.152) | copy-start | bytes 12292
  135.6 9.2 %copy-start.11 = (f32[16,8,8]{0,2,1:T(8,128)S(1)}, f32[16,8,8]{0,2,1:T(8,128)}, u32[]{:S(2)}) copy-start(f32[16,8,8]{0,2,1:T(8,128)} %get-tuple-element.149) | copy-start | bytes 12292
  140.6 2.7 %copy-start.13 = (f32[16,8,8]{0,2,1:T(8,128)S(1)}, f32[16,8,8]{0,2,1:T(8,128)}, u32[]{:S(2)}) copy-start(f32[16,8,8]{0,2,1:T(8,128)} %get-tuple-element.151) | copy-start | bytes 12292
  141.3 1.2 copy-start.14
  142.6 3.6 %copy-start.2 = (bf16[16,8,8,512]{3,0,2,1:T(8,128)(2,1)S(1)}, bf16[16,8,8,512]{3,0,2,1:T(8,128)(2,1)}, u32[]{:S(2)}) copy-start(bf16[16,8,8,512]{3,0,2,1:T(8,128)(2,1)} %get-tuple-element.165) | copy-start | bytes 3145732
  144.0 2.2 %copy-start.15 = (f32[16,8,8]{2,0,1:T(8,128)S(1)}, f32[16,8,8]{2,0,1:T(8,128)}, u32[]{:S(2)}) copy-start(f32[16,8,8]{2,0,1:T(8,128)} %copy.137) | copy-start | bytes 12292
  145.4 1.2 copy-start.3
  145.4 1.2 copy-start.16
  145.4 1.2 copy-start.17
  145.4 1.2 copy-start.19
  145.4 1.2 copy-start.22
  146.7 1.6 %copy-start.1 = (bf16[128,8,8,128]{3,2,1,0:T(8,128)(2,1)S(1)}, bf16[128,8,8,128]{3,2,1,0:T(8,128)(2,1)}, u32[]{:S(2)}) copy-start(bf16[128,8,8,128]{3,2,1,0:T(8,128)(2,1)} %copy.197) | copy-start | bytes 6291460
  146.7 1.6 %copy-start.7 = (bf16[16,8,8,64]{3,2,1,0:T(8,128)(2,1)S(1)}, bf16[16,8,8,64]{3,2,1,0:T(8,128)(2,1)}, u32[]{:S(2)}) copy-start(bf16[16,8,8,64]{3,2,1,0:T(8,128)(2,1)} %get-tuple-element.168) | copy-start | bytes 393220
  146.7 1.6 %copy-start.18 = (f32[16,8,8]{2,0,1:T(8,128)S(1)}, f32[16,8,8]{2,0,1:T(8,128)}, u32[]{:S(2)}) copy-start(f32[16,8,8]{2,0,1:T(8,128)} %copy.149) | copy-start | bytes 12292
  146.7 1.6 %copy-start.20 = (f32[16,8,8]{2,0,1:T(8,128)S(1)}, f32[16,8,8]{2,0,1:T(8,128)}, u32[]{:S(2)}) copy-start(f32[16,8,8]{2,0,1:T(8,128)} %copy.151) | copy-start | bytes 12292
  146.7 1.6 %copy-start.21 = (f32[16,8,8]{2,0,1:T(8,128)S(1)}, f32[16,8,8]{2,0,1:T(8,128)}, u32[]{:S(2)}) copy-start(f32[16,8,8]{2,0,1:T(8,128)} %copy.153) | copy-start | bytes 12292
  146.7 1.6 %copy-start.23 = (f32[16,8,8]{2,0,1:T(8,128)S(1)}, f32[16,8,8]{2,0,1:T(8,128)}, u32[]{:S(2)}) copy-start(f32[16,8,8]{2,0,1:T(8,128)} %copy.159) | copy-start | bytes 12292
  146.7 1.6 %copy-start.25 = (f32[16,8,128]{2,0,1:T(8,128)S(1)}, f32[16,8,128]{2,0,1:T(8,128)}, u32[]{:S(2)}) copy-start(f32[16,8,128]{2,0,1:T(8,128)} %copy.152) | copy-start | bytes 196612
Sparse Core Ops, SparseCore 0:
  8.9 30.6 all-gather.2
  41.1 22.1 all-gather.4
